TPU v7x, 32 devices: a whole 2x2x4 slice. The times are simulated.
32 devices in a mesh: mem: 4 (over x, core), grid: 8 (over z, y).
Axes of the slice: x: 2, y: 2, z: 4, core: 2. Of those that a mesh axis runs over, the one named last changes fastest.
Arguments:
- obs_ensemble: bfloat16 [256, 32, 256], P('mem', 'grid'), may hold values from -6 to 6
- obs_values: bfloat16 [32, 256], P('grid'), may hold values from -6 to 6
- inverse_error: bfloat16 [32, 256], P('grid'), may hold values from 0.5 to 8
- obs_counts: int32 [32], P('grid'), may hold values from 1 to 256, as said below
- loc_offsets: int32 [32, 4], P('grid'), may hold values from -2 to 2, as said below
- background: bfloat16 [256, 256, 320], P('mem', 'grid'), may hold values from -6 to 6
Outputs:
- analysis: bfloat16 [256, 256, 320], P('mem', 'grid')
Inputs may be any that keep to these rules, and one draw needn't show every extreme that they name: `obs_counts`: counts up to about five times their mean; some block in every draw is full. `loc_offsets`: entry 0 of every list is 0 (the block's own observations); the other entries of a list are distinct nonzero offsets.
All inputs are finite; a program needn't handle non-finite values.
Results may differ from a plain program's by a relative error of at most 0.0063.
Values may be sent and summed in bfloat16 or wider, within the bound.
A program may use at most 128 MiB of HBM per device.

v0:
```python
import jax
import jax.numpy as jnp
from jax import lax
from jax.sharding import PartitionSpec as P

MEMBERS = 256
BLOCK_COLS = 8
REACH = 2
LOC_LEN = 4
NS_STEPS = 6


def padded(x, sides, width):
    for axis, dim in sides:
        count, length = (lax.axis_size(axis), x.shape[dim])
        up = [(i, (i + 1) % count) for i in range(count)]
        down = [(j, i) for i, j in up]
        last = lax.slice_in_dim(x, length - width, length, axis=dim)
        initial = lax.slice_in_dim(x, 0, width, axis=dim)
        before = lax.ppermute(last, axis, up)
        after = lax.ppermute(initial, axis, down)
        x = jnp.concatenate([before, x, after], axis=dim)
    return x


def taper_of(offsets):
    return 1.0 / (1.0 + jnp.abs(offsets).astype(jnp.float32))


def block_weights(members, obs_row, weight_row):
    members_wide = members.astype(jnp.float32)
    obs_mean = jnp.mean(members_wide, axis=0)
    scaled = ((members_wide - obs_mean) * weight_row).astype(jnp.bfloat16)
    innovation = (obs_row - obs_mean) * weight_row
    gram = jnp.dot(scaled, scaled.T, preferred_element_type=jnp.float32)
    rhs = jnp.dot(scaled.astype(jnp.float32), innovation, precision=lax.Precision.HIGHEST)
    identity = jnp.eye(MEMBERS, dtype=jnp.float32)
    system = identity + gram / (MEMBERS - 1)
    scale = jnp.sqrt(jnp.sum(system * system))
    upper = system / scale
    lower = identity
    for step in range(NS_STEPS):
        middle = 0.5 * (3.0 * identity - jnp.dot(lower, upper, precision=lax.Precision.HIGHEST))
        upper = jnp.dot(upper, middle, precision=lax.Precision.HIGHEST)
        lower = jnp.dot(middle, lower, precision=lax.Precision.HIGHEST)
    root_inv = lower / jnp.sqrt(scale)
    inner = jnp.dot(root_inv, rhs, precision=lax.Precision.HIGHEST)
    shift = jnp.dot(root_inv, inner, precision=lax.Precision.HIGHEST) / (MEMBERS - 1)
    return (root_inv + shift[:, None]).astype(jnp.bfloat16)


def apply_weights(weights, state):
    state_wide = state.astype(jnp.float32)
    state_mean = jnp.mean(state_wide, axis=0)
    perturbation = (state_wide - state_mean).astype(jnp.bfloat16)
    product = jnp.einsum("bkj,kbv->jbv", weights, perturbation, preferred_element_type=jnp.float32)
    return (state_mean + product).astype(jnp.bfloat16)


def on_device(obs_ensemble, obs_values, inverse_error, obs_counts, loc_offsets, background):
    local_members, dev_blocks, slots = obs_ensemble.shape
    mem_count = lax.axis_size("mem")
    per_device = dev_blocks // mem_count
    list_width = LOC_LEN * slots
    slot_ids = jnp.arange(slots, dtype=jnp.int32)
    valid = (slot_ids[None, :] < obs_counts[:, None]).astype(jnp.float32)
    masked = (inverse_error.astype(jnp.float32) * valid).astype(jnp.bfloat16)
    stacked = jnp.concatenate([obs_ensemble, obs_values[None], masked[None]], axis=0)
    extended = padded(stacked, (("grid", 1),), REACH)
    chosen = (jnp.arange(dev_blocks, dtype=jnp.int32)[:, None] + REACH + loc_offsets).reshape(-1)
    picked = jnp.take(extended, chosen, axis=1).reshape(local_members + 2, dev_blocks, list_width)
    member_part = picked[:local_members].reshape(local_members, mem_count, per_device, list_width)
    mem_rank = lax.axis_index("mem")
    first_block = mem_rank * per_device
    table_part = lax.dynamic_slice_in_dim(picked[local_members:], first_block, per_device, 1)
    own_taper = lax.dynamic_slice_in_dim(taper_of(loc_offsets), first_block, per_device, 0)
    taper_rows = jnp.repeat(own_taper, slots, axis=1)
    received = lax.all_to_all(member_part, "mem", split_axis=1, concat_axis=0, tiled=True)
    received = received.reshape(MEMBERS, per_device, list_width)
    weight_rows = table_part[1].astype(jnp.float32) * taper_rows
    weights = jax.vmap(block_weights, in_axes=(1, 0, 0))(
        received, table_part[0].astype(jnp.float32), weight_rows
    )
    dev_cols = background.shape[1]
    variables = background.shape[2]
    pieces = background.reshape(local_members, mem_count, per_device * BLOCK_COLS, variables)
    moved = lax.all_to_all(pieces, "mem", split_axis=1, concat_axis=0, tiled=True)
    moved = moved.reshape(MEMBERS, per_device, BLOCK_COLS * variables)
    updated = apply_weights(weights, moved)
    updated = updated.reshape(MEMBERS, 1, per_device * BLOCK_COLS, variables)
    returned = lax.all_to_all(updated, "mem", split_axis=0, concat_axis=1, tiled=True)
    return returned.reshape(local_members, dev_cols, variables)


def solution(mesh):
    placed = (
        P("mem", "grid", None),
        P("grid", None),
        P("grid", None),
        P("grid"),
        P("grid", None),
        P("mem", "grid", None),
    )
    return jax.shard_map(
        on_device, mesh=mesh, in_specs=placed, out_specs=P("mem", "grid", None), check_vma=False
    )
```

profile of v0, /device:TPU:1, one launch (start us, length us, event | category | flops | bytes accessed | tf_op | source)
XLA Modules:
  0.0 81.5 jit_solution(6703048874097502343)
XLA Ops:
  0.0 0.8 fusion.21
  0.8 0.7 copy.22
  1.4 0.9 %copy.21 = bf16[64,4,256]{2,0,1:T(8,128)(2,1)S(1)} copy(bf16[64,4,256]{2,1,0:T(4,128)(2,1)} %param.6) | data formatting | bytes 262144 | tf_op args[0]
  2.4 2.1 %collective-permute-start = (bf16[66,2,256]{2,0,1:T(8,128)(2,1)S(1)}, bf16[66,2,256]{2,0,1:T(8,128)(2,1)S(1)}, u32[]{:S(2)}, u32[]{:S(2)}) collective-permute-start(bf16[66,2,256]{2,0,1:T(8,128)(2,1)S(1)} %get-tuple-element.5), channel_id=1, source_target_pairs={{0,1},{1,2},{2,3},{3,4},{4,5},{5,6},{6,7},{7,0},{8,9},{9,10},{10,1... | collective-permute-start | bytes 202760 | tf_op jit(solution)/shard_map/ppermute | solution.py:20
  4.5 3.1 %collective-permute-start.1 = (bf16[66,2,256]{2,0,1:T(8,128)(2,1)S(1)}, bf16[66,2,256]{2,0,1:T(8,128)(2,1)S(1)}, u32[]{:S(2)}, u32[]{:S(2)}) collective-permute-start(bf16[66,2,256]{2,0,1:T(8,128)(2,1)S(1)} %get-tuple-element.6), channel_id=1, source_target_pairs={{1,0},{2,1},{3,2},{4,3},{5,4},{6,5},{7,6},{0,7},{9,8},{10,9},{11,1... | collective-permute-start | bytes 202760 | tf_op jit(solution)/shard_map/ppermute | solution.py:21
  7.6 0.8 broadcast_add_fusion
  8.4 0.1 reshape.379
  8.5 0.1 reshape.378
  8.6 0.8 %collective-permute-done = bf16[66,2,256]{2,0,1:T(8,128)(2,1)S(1)} collective-permute-done((bf16[66,2,256]{2,0,1:T(8,128)(2,1)S(1)}, bf16[66,2,256]{2,0,1:T(8,128)(2,1)S(1)}, u32[]{:S(2)}, u32[]{:S(2)}) %collective-permute-start) | collective-permute-done | bytes 67616 | tf_op jit(solution)/shard_map/ppermute | solution.py:20
  9.4 0.0 collective-permute-done.1
  9.4 0.6 gather_fusion
  10.0 0.1 select_bitcast_fusion
  10.2 0.3 copy.24
  10.5 0.0 copy-start
  10.5 0.2 reshape.380
  10.7 0.9 %copy.25 = bf16[64,4,1,1024]{3,0,2,1:T(8,128)(2,1)} copy(bf16[64,4,1,1024]{3,1,0,2:T(4,128)(2,1)S(1)} %reshape.380) | data formatting | bytes 1048576 | tf_op jit(solution)/shard_map/reshape | solution.py:72
  11.7 5.4 %all-to-all-start.1 = ((bf16[64,4,1,1024]{3,0,2,1:T(8,128)(2,1)}), bf16[64,4,1,1024]{3,0,2,1:T(8,128)(2,1)S(1)}, u32[]{:S(2)}, u32[]{:S(2)}) async-start(bf16[64,4,1,1024]{3,0,2,1:T(8,128)(2,1)} %copy.25), calls=%async_computation.1 | async-start | bytes 1048576 | tf_op jit(solution)/shard_map/all_to_all | solution.py:78
  17.1 0.0 copy-done
  17.2 0.1 broadcast_in_dim.22
  17.2 2.7 %copy.20 = bf16[64,4,8,320]{3,2,0,1:T(8,128)(2,1)} copy(bf16[64,4,8,320]{3,2,1,0:T(8,128)(2,1)} %bitcast.102) | data formatting | bytes 2621440 | tf_op jit(solution)/shard_map/reshape | solution.py:86
  20.0 4.9 %all-to-all-done.1 = bf16[64,4,1,1024]{3,0,2,1:T(8,128)(2,1)S(1)} async-done(((bf16[64,4,1,1024]{3,0,2,1:T(8,128)(2,1)}), bf16[64,4,1,1024]{3,0,2,1:T(8,128)(2,1)S(1)}, u32[]{:S(2)}, u32[]{:S(2)}) %all-to-all-start.1) | async-done | bytes 524320 | tf_op jit(solution)/shard_map/all_to_all | solution.py:78
  25.0 4.5 %all-to-all-start = ((bf16[64,4,8,320]{3,2,0,1:T(8,128)(2,1)}), bf16[64,4,8,320]{3,2,0,1:T(8,128)(2,1)S(1)}, u32[]{:S(2)}, u32[]{:S(2)}) async-start(bf16[64,4,8,320]{3,2,0,1:T(8,128)(2,1)} %copy.20), calls=%async_computation | async-start | bytes 3145728 | tf_op jit(solution)/shard_map/all_to_all | solution.py:87
  29.5 0.1 convert_reduce_fusion.1
  29.6 0.1 fusion.12
  29.7 0.9 %multiply_reduce_fusion = (f32[]{:T(128)}, f32[256,256]{1,0:T(8,128)S(1)}) fusion(bf16[256,1024]{1,0:T(8,128)(2,1)S(1)} %bitcast.100), kind=kOutput, calls=%fused_computation.34 | convolution fusion | flops 134610944 | bytes 786436 | tf_op jit(solution)/shard_map/vmap()/dot_general | solution.py:35
  31.3 0.3 fusion.8
  31.6 0.4 fusion.15
  32.0 0.3 fusion.13
  32.3 0.4 fusion.7
  32.6 0.4 fusion.27
  33.0 0.4 fusion.26
  33.4 0.4 fusion.6
  33.8 0.4 fusion.29
  34.2 0.4 fusion.28
  34.6 0.4 fusion.5
  35.0 0.4 fusion.31
  35.4 0.4 fusion.30
  35.7 0.4 fusion.4
  36.1 0.4 fusion.32
  36.5 0.4 fusion.33
  36.9 0.4 fusion.3
  37.3 0.5 convolution_bitcast_fusion.2
  37.9 0.4 convolution_divide_fusion
  38.3 0.3 convolution_bitcast_fusion.1
  38.5 0.3 fusion.34
  38.9 9.7 %all-to-all-done = bf16[64,4,8,320]{3,2,0,1:T(8,128)(2,1)S(1)} async-done(((bf16[64,4,8,320]{3,2,0,1:T(8,128)(2,1)}), bf16[64,4,8,320]{3,2,0,1:T(8,128)(2,1)S(1)}, u32[]{:S(2)}, u32[]{:S(2)}) %all-to-all-start) | async-done | bytes 1310752 | tf_op jit(solution)/shard_map/all_to_all | solution.py:87
  48.6 0.3 convert_reduce_fusion
  48.9 0.1 div.51
  48.9 1.9 %convert_bitcast_fusion = f32[4,64,1,8,320]{4,3,1,0,2:T(8,128)} fusion(bf16[64,4,8,320]{3,2,0,1:T(8,128)(2,1)S(1)} %all-to-all-done), kind=kLoop, calls=%fused_computation.3 | loop fusion | flops 655360 | bytes 3932160 | tf_op jit(solution)/shard_map/convert_element_type | solution.py:53
  50.8 2.9 %reshape.383 = f32[256,2560]{1,0:T(8,128)S(1)} reshape(f32[4,64,1,8,320]{4,3,1,0,2:T(8,128)} %convert_bitcast_fusion) | data formatting | bytes 5242880 | tf_op jit(solution)/shard_map/convert_element_type | solution.py:53
  53.7 1.9 %fusion.1 = bf16[1,2560,256]{2,1,0:T(8,128)(2,1)} fusion(f32[256,2560]{1,0:T(8,128)S(1)} %reshape.383, f32[2560]{0:T(1024)S(1)} %div.51, f32[256,256]{1,0:T(8,128)S(1)} %convolution_divide_fusion, f32[256]{0:T(256)S(1)} %broadcast_multiply_fusion.2), kind=kOutput, calls=%fused_computation.5 | convolution fusion | flops 338296832 | bytes 4205568 | tf_op jit(solution)/shard_map/bkj,kbv->jbv/dot_general | solution.py:56
  55.6 2.1 %copy.28 = bf16[256,1,8,320]{3,2,1,0:T(8,128)(2,1)S(1)} copy(bf16[256,1,8,320]{0,3,2,1:T(8,128)(2,1)} %bitcast.99) | data formatting | bytes 2621440 | tf_op jit(solution)/shard_map/reshape | solution.py:90
  57.7 22.4 %all_to_all.33 = bf16[256,1,8,320]{3,2,1,0:T(8,128)(2,1)S(1)} all-to-all(bf16[256,1,8,320]{3,2,1,0:T(8,128)(2,1)S(1)} %copy.28), channel_id=1, replica_groups=mesh['mem'=4,'grid'=8] {'mem'}, dimensions={0} | all-to-all | bytes 2621440 | tf_op jit(solution)/shard_map/all_to_all | solution.py:91
  80.2 1.3 %copy.31 = bf16[64,4,1,8,320]{4,3,1,0,2:T(8,128)(2,1)} copy(bf16[64,4,1,8,320]{4,3,0,1,2:T(8,128)(2,1)S(1)} %bitcast.98) | data formatting | bytes 2621440 | tf_op jit(solution)/shard_map/all_to_all | solution.py:91
  (19 shorter events, 0.2 us)
Async XLA Ops:
  2.4 7.0 %collective-permute-start = (bf16[66,2,256]{2,0,1:T(8,128)(2,1)S(1)}, bf16[66,2,256]{2,0,1:T(8,128)(2,1)S(1)}, u32[]{:S(2)}, u32[]{:S(2)}) collective-permute-start(bf16[66,2,256]{2,0,1:T(8,128)(2,1)S(1)} %get-tuple-element.5), channel_id=1, source_target_pairs={{0,1},{1,2},{2,3},{3,4},{4,5},{5,6},{6,7},{7,0},{8,9},{9,10},{10,1... | collective-permute-start | bytes 202760 | tf_op jit(solution)/shard_map/ppermute | solution.py:20
  4.5 4.9 %collective-permute-start.1 = (bf16[66,2,256]{2,0,1:T(8,128)(2,1)S(1)}, bf16[66,2,256]{2,0,1:T(8,128)(2,1)S(1)}, u32[]{:S(2)}, u32[]{:S(2)}) collective-permute-start(bf16[66,2,256]{2,0,1:T(8,128)(2,1)S(1)} %get-tuple-element.6), channel_id=1, source_target_pairs={{1,0},{2,1},{3,2},{4,3},{5,4},{6,5},{7,6},{0,7},{9,8},{10,9},{11,1... | collective-permute-start | bytes 202760 | tf_op jit(solution)/shard_map/ppermute | solution.py:21
  10.5 6.6 %copy-start = (s32[4,4]{1,0:T(4,128)S(1)}, s32[4,4]{1,0:T(4,128)}, u32[]{:S(2)}) copy-start(s32[4,4]{1,0:T(4,128)} %param.10) | copy-start | bytes 196
  11.7 13.3 %all-to-all-start.1 = ((bf16[64,4,1,1024]{3,0,2,1:T(8,128)(2,1)}), bf16[64,4,1,1024]{3,0,2,1:T(8,128)(2,1)S(1)}, u32[]{:S(2)}, u32[]{:S(2)}) async-start(bf16[64,4,1,1024]{3,0,2,1:T(8,128)(2,1)} %copy.25), calls=%async_computation.1 | async-start | bytes 1048576 | tf_op jit(solution)/shard_map/all_to_all | solution.py:78
  25.0 23.6 %all-to-all-start = ((bf16[64,4,8,320]{3,2,0,1:T(8,128)(2,1)}), bf16[64,4,8,320]{3,2,0,1:T(8,128)(2,1)S(1)}, u32[]{:S(2)}, u32[]{:S(2)}) async-start(bf16[64,4,8,320]{3,2,0,1:T(8,128)(2,1)} %copy.20), calls=%async_computation | async-start | bytes 3145728 | tf_op jit(solution)/shard_map/all_to_all | solution.py:87
where the time goes:
time: 83 us; the launch traced here: 81.5 us
  blocking collectives  22.4 us (27%)
  waiting for transfers between devices  15.5 us (19%)
  starting transfers between devices  15.2 us (18%)
  local copies, waits for them, and re-layouts  13.1 us (16%)
  matrix products  10.2 us (12%)
  other arithmetic  4.13 us (5%)
  between operations  0.97 us (1%)
    all_to_all x1, blocking collectives, on_device(): lax.all_to_all(updated, 'mem', split_axis=0, concat_axis=1, tiled=True)  22.4 us
    all_to_all x1, waiting for transfers between devices, on_device(): lax.all_to_all(pieces, 'mem', split_axis=1, concat_axis=0, tiled=True)  9.7 us
    all_to_all x1, starting transfers between devices, on_device(): lax.all_to_all(member_part, 'mem', split_axis=1, concat_axis=0, tiled=True)  5.44 us
    all_to_all x1, waiting for transfers between devices, on_device(): lax.all_to_all(member_part, 'mem', split_axis=1, concat_axis=0, tiled=True)  4.95 us
    all_to_all x1, starting transfers between devices, on_device(): lax.all_to_all(pieces, 'mem', split_axis=1, concat_axis=0, tiled=True)  4.5 us
    ppermute x1, starting transfers between devices, padded(): after = lax.ppermute(initial, axis, down)  3.1 us
    convert_element_type x1, local copies, waits for them, and re-layouts, apply_weights(): state_wide = state.astype(jnp.float32)  2.9 us
    reshape x1, local copies, waits for them, and re-layouts, on_device(): background.reshape(local_members, mem_count, per_device * BLOCK_COLS, var...  2.71 us
  transfers between devices with their start and end apart: 4, of which 3 were waited for; matrix products, arithmetic and copies ran while one was open for 15% of the time, Pallas kernels for 0%

commit v1 on v0

v1 whole, which is shorter than its diff:
```python
import functools

import jax
import jax.numpy as jnp
from jax import lax
from jax.experimental import pallas as pl
from jax.experimental.pallas import tpu as pltpu
from jax.sharding import PartitionSpec as P

BLOCK_COLS = 8
REACH = 2
NS_STEPS = 6
MESH = pl.DeviceIdType.MESH
HIGHEST = lax.Precision.HIGHEST
NT = (((1,), (1,)), ((), ()))


def dot(a, b):
    return jnp.dot(a, b, precision=HIGHEST, preferred_element_type=jnp.float32)


def kernel(n, grid_n, loc_len, chunks, loc_ref, taper_ref, obs_ref, table_ref, bg_ref, out_ref,
           near, tables, state, upper, lower, sent_w, got_w,
           obs_send, obs_recv, tab_send, tab_recv, own_sem, direct_send, pair_send, pass_send, state_recv,
           w_send, w_recv):
    me = lax.axis_index("mem")
    row = lax.axis_index("grid")
    core = lax.rem(me, 2)
    sibling = me + 1 - 2 * core
    blocks, local, slots = obs_ref.shape
    members = n * local
    width = bg_ref.shape[1]
    step = width // chunks
    rest = n // 2

    def at(mem, shift):
        return {"mem": mem, "grid": lax.rem(row + shift + grid_n, grid_n)}

    barrier = pltpu.get_barrier_semaphore()
    for shift in (0, -1, 1):
        for k in range(0 if shift else 1, n):
            pl.semaphore_signal(barrier, inc=1, device_id=at(lax.rem(me + k, n), shift), device_id_type=MESH)
    own_rows = pl.ds(pl.multiple_of(me * local, local), local)
    own_state = pltpu.make_async_copy(bg_ref, state.at[own_rows], own_sem.at[0])
    own_state.start()
    own_table = pltpu.make_async_copy(table_ref, tables.at[pl.ds(blocks, blocks)], own_sem.at[1])
    own_table.start()
    pl.semaphore_wait(barrier, 3 * n - 1)

    def obs_copy(i, e):
        target = i + e
        return pltpu.make_async_remote_copy(
            src_ref=obs_ref.at[i], dst_ref=near.at[REACH - e, own_rows],
            send_sem=obs_send.at[i, e + REACH], recv_sem=obs_recv.at[REACH - e, me],
            device_id=at(target % n, target // n), device_id_type=MESH)

    def table_copy(side):
        place = 0 if side == 1 else 2 * blocks
        return pltpu.make_async_remote_copy(
            src_ref=table_ref, dst_ref=tables.at[pl.ds(place, blocks)],
            send_sem=tab_send.at[(side + 1) // 2], recv_sem=tab_recv.at[(side + 1) // 2],
            device_id=at(me, side), device_id_type=MESH)

    for side in (-1, 1):
        table_copy(side).start()
    order = [(i, e) for i in range(blocks) for e in range(-REACH, REACH + 1)]
    order.sort(key=lambda p: 0 <= p[0] + p[1] < n)
    for i, e in order:
        target = i + e
        if 0 <= target < n:
            @pl.when(me != target)
            def _():
                obs_copy(i, e).start()

            @pl.when(me == target)
            def _():
                pltpu.make_async_copy(obs_ref.at[i], near.at[REACH - e, own_rows],
                                      obs_recv.at[REACH - e, me]).start()
        else:
            obs_copy(i, e).start()

    def piece(j):
        return pl.ds(j * step, step)

    def direct(k, j):
        peer = lax.rem(me + 2 * k, n)
        return pltpu.make_async_remote_copy(
            src_ref=bg_ref.at[:, piece(j)], dst_ref=state.at[own_rows, piece(j)],
            send_sem=direct_send.at[k, j], recv_sem=state_recv.at[me, j],
            device_id=at(peer, 0), device_id_type=MESH)

    def paired(j):
        return pltpu.make_async_remote_copy(
            src_ref=bg_ref.at[:, piece(j)], dst_ref=state.at[own_rows, piece(j)],
            send_sem=pair_send.at[j], recv_sem=state_recv.at[me, j],
            device_id=at(sibling, 0), device_id_type=MESH)

    def passed(k, j):
        source = lax.rem(me + n - 2 * k, n)
        rows = pl.ds(pl.multiple_of(source * local, local), local)
        return pltpu.make_async_remote_copy(
            src_ref=state.at[rows, piece(j)], dst_ref=state.at[rows, piece(j)],
            send_sem=pass_send.at[k, j], recv_sem=state_recv.at[source, j],
            device_id=at(sibling, 0), device_id_type=MESH)

    def await_state(source, j):
        rows = pl.ds(pl.multiple_of(source * local, local), local)
        ref = state.at[rows, piece(j)]
        pltpu.make_async_copy(ref, ref, state_recv.at[source, j]).wait()

    for j in range(chunks):
        for k in range(1, rest):
            direct(k, j).start()
        paired(j).start()

    own_state.wait()
    own_table.wait()
    for side in (-1, 1):
        table_copy(side).wait_recv()
    for s in range(2 * REACH + 1):
        for source in range(n):
            ref = near.at[s, pl.ds(source * local, local)]
            pltpu.make_async_copy(ref, ref, obs_recv.at[s, source]).wait()

    gram = jnp.zeros((members, members), jnp.float32)
    rhs = jnp.zeros((8, members), jnp.float32)
    for j in range(loc_len):
        offset = loc_ref[me, j]
        wide = near[offset + REACH].astype(jnp.float32)
        table = tables[blocks + me + offset]
        weight = table[1:2] * taper_ref[me, j]
        mean = jnp.sum(wide, axis=0, keepdims=True) * (1.0 / members)
        scaled = ((wide - mean) * weight).astype(jnp.bfloat16)
        innovation = jnp.broadcast_to((table[0:1] - mean) * weight, (8, slots))
        gram = gram + lax.dot_general(scaled, scaled, NT, preferred_element_type=jnp.float32)
        rhs = rhs + lax.dot_general(innovation, scaled.astype(jnp.float32), NT, precision=HIGHEST,
                                    preferred_element_type=jnp.float32)
    across = lax.broadcasted_iota(jnp.int32, (members, members), 0)
    along = lax.broadcasted_iota(jnp.int32, (members, members), 1)
    identity = (across == along).astype(jnp.float32)
    system = identity + gram / (members - 1)
    square = jnp.sum(jnp.sum(system * system, axis=1, keepdims=True), axis=0, keepdims=True)
    scale = jnp.sqrt(square)
    first = system / scale
    middle = 0.5 * (3.0 * identity - first)
    upper[...] = dot(first, middle)
    lower[...] = middle

    def newton(_, carry):
        mid = 1.5 * identity - 0.5 * dot(lower[...], upper[...])
        upper[...] = dot(upper[...], mid)
        lower[...] = dot(mid, lower[...])
        return carry

    lax.fori_loop(0, NS_STEPS - 2, newton, 0)
    middle = 1.5 * identity - 0.5 * dot(lower[...], upper[...])
    root_inv = dot(middle, lower[...]) / jnp.sqrt(scale)
    shift = dot(dot(rhs, root_inv), root_inv) / (members - 1)
    weights = (root_inv + shift[0:1]).astype(jnp.bfloat16).astype(jnp.float32)
    weights = weights - jnp.sum(weights, axis=1, keepdims=True) * (1.0 / members) + 1.0 / members
    high = weights.astype(jnp.bfloat16)
    low = (weights - high.astype(jnp.float32)).astype(jnp.bfloat16)
    sent_w[0] = high
    sent_w[1] = low

    for k in range(1, rest):
        await_state(lax.rem(me + n - 2 * k, n), 0)
        passed(k, 0).start()

    def weight_copy(k):
        peer = lax.rem(me + k, n)
        return pltpu.make_async_remote_copy(
            src_ref=sent_w.at[:, pl.ds(pl.multiple_of(peer * local, local), local)], dst_ref=got_w.at[me],
            send_sem=w_send.at[k], recv_sem=w_recv.at[me], device_id=at(peer, 0), device_id_type=MESH)

    for k in range(1, n):
        weight_copy(k).start()
    own_w = pltpu.make_async_copy(sent_w.at[:, own_rows], got_w.at[me], w_recv.at[me])
    own_w.start()
    for source in range(n):
        pltpu.make_async_copy(got_w.at[source], got_w.at[source], w_recv.at[source]).wait()

    per_block = width // blocks
    for j in range(chunks):
        if j + 1 < chunks:
            for k in range(1, rest):
                await_state(lax.rem(me + n - 2 * k, n), j + 1)
                passed(k, j + 1).start()
        await_state(sibling, j)
        for k in range(1, rest):
            await_state(lax.rem(sibling + n - 2 * k, n), j)
        block = j * step // per_block
        block_state = state[:, piece(j)]
        total = jnp.dot(got_w[block, 0], block_state, preferred_element_type=jnp.float32)
        total = total + jnp.dot(got_w[block, 1], block_state, preferred_element_type=jnp.float32)
        out_ref[:, piece(j)] = total.astype(jnp.bfloat16)

    for i, e in order:
        target = i + e
        if 0 <= target < n:
            @pl.when(me != target)
            def _():
                obs_copy(i, e).wait_send()
        else:
            obs_copy(i, e).wait_send()
    for side in (-1, 1):
        table_copy(side).wait_send()
    for k in range(1, n):
        weight_copy(k).wait_send()
    for j in range(chunks):
        paired(j).wait_send()
        for k in range(1, rest):
            direct(k, j).wait_send()
            passed(k, j).wait_send()


def on_device(n, grid_n, obs_ensemble, obs_values, inverse_error, obs_counts, loc_offsets, background):
    local, blocks, slots = obs_ensemble.shape
    cols, variables = background.shape[1:]
    members = n * local
    loc_len = loc_offsets.shape[1]
    width = cols * variables
    chunks = 2 * blocks
    assert blocks == n and n % 2 == 0
    slot_ids = jnp.arange(slots, dtype=jnp.int32)
    masked = jnp.where(slot_ids[None, :] < obs_counts[:, None], inverse_error.astype(jnp.float32), 0.0)
    table = jnp.stack([obs_values.astype(jnp.float32), masked], axis=1)
    table = jnp.pad(table, ((0, 0), (0, 6), (0, 0)))
    taper = 1.0 / (1.0 + jnp.abs(loc_offsets).astype(jnp.float32))
    dma = pltpu.SemaphoreType.DMA
    smem = pl.BlockSpec(memory_space=pltpu.SMEM)
    vmem = pl.BlockSpec(memory_space=pltpu.VMEM)
    out = pl.pallas_call(
        functools.partial(kernel, n, grid_n, loc_len, chunks),
        out_shape=jax.ShapeDtypeStruct((local, width), jnp.bfloat16),
        in_specs=[smem, smem, vmem, vmem, vmem],
        out_specs=vmem,
        scratch_shapes=[
            pltpu.VMEM((2 * REACH + 1, members, slots), jnp.bfloat16),
            pltpu.VMEM((3 * blocks, 8, slots), jnp.float32),
            pltpu.VMEM((members, width), jnp.bfloat16),
            pltpu.VMEM((members, members), jnp.float32),
            pltpu.VMEM((members, members), jnp.float32),
            pltpu.VMEM((2, members, members), jnp.bfloat16),
            pltpu.VMEM((n, 2, local, members), jnp.bfloat16),
            dma((blocks, 2 * REACH + 1)),
            dma((2 * REACH + 1, n)),
            dma((2,)),
            dma((2,)),
            dma((2,)),
            dma((n // 2, chunks)),
            dma((chunks,)),
            dma((n // 2, chunks)),
            dma((n, chunks)),
            dma((n,)),
            dma((n,)),
        ],
        compiler_params=pltpu.CompilerParams(collective_id=0, has_side_effects=True, vmem_limit_bytes=60 * 2**20),
        name="analysis",
    )(loc_offsets, taper, obs_ensemble.transpose(1, 0, 2), table, background.reshape(local, width))
    return out.reshape(local, cols, variables)


def solution(mesh):
    placed = (
        P("mem", "grid", None),
        P("grid", None),
        P("grid", None),
        P("grid"),
        P("grid", None),
        P("mem", "grid", None),
    )
    body = functools.partial(on_device, mesh.shape["mem"], mesh.shape["grid"])
    return jax.shard_map(body, mesh=mesh, in_specs=placed, out_specs=P("mem", "grid", None), check_vma=False)
```

time: 83 us -> 68.9 us (0.83); the launches traced: 81.5 us -> 68.6 us
  Pallas kernels: 0 us -> 55.6 us
  blocking collectives: 22.4 us -> 0 us
  waiting for transfers between devices: 15.5 us -> 0 us
  starting transfers between devices: 15.2 us -> 0 us
  matrix products: 10.2 us -> 0 us
  local copies, waits for them, and re-layouts: 13.1 us -> 10.3 us
  other arithmetic: 4.13 us -> 2.63 us
  between operations: 0.97 us -> 0.01 us
    pallas_call x0 -> x1, Pallas kernels: none -> 55.6 us  [on_device(): pl.pallas_call(functools.partial(kernel, n, grid_n, loc_len, chunks), out...]
    all_to_all x1 -> x0, blocking collectives: 22.4 us -> none  [on_device(): lax.all_to_all(updated, 'mem', split_axis=0, concat_axis=1, tiled=True)]
    all_to_all x2 -> x0, waiting for transfers between devices: 14.6 us -> none  [the longest x1 9.7 us: on_device(): lax.all_to_all(pieces, 'mem', split_axis=1, concat_axis=0, tiled=True)]
    dot_general x22 -> x0, matrix products: 10.2 us -> none  [the longest x6 2.22 us: block_weights(): jnp.dot(lower, upper, precision=lax.Precision.HIGHEST)]
    all_to_all x2 -> x0, starting transfers between devices: 9.94 us -> none  [the longest x1 5.44 us: on_device(): lax.all_to_all(member_part, 'mem', split_axis=1, concat_axis=0, tiled=True)]
    ppermute x2 -> x0, starting transfers between devices: 5.21 us -> none  [the longest x1 3.1 us: padded(): after = lax.ppermute(initial, axis, down)]
    convert_element_type x1 -> x0, local copies, waits for them, and re-layouts: 2.9 us -> none  [apply_weights(): state_wide = state.astype(jnp.float32)]
    convert_element_type x2 -> x0, other arithmetic: 2 us -> none  [the longest x1 1.87 us: apply_weights(): state_wide = state.astype(jnp.float32)]
  transfers between devices with their start and end apart: 4 -> 0, of which waited for: 3 -> 0; matrix products, arithmetic and copies ran while one was open for 15% -> 0% of each run, Pallas kernels for 0% -> 0%
where the time goes in v1:
time: 68.9 us; the launch traced here: 68.6 us
  Pallas kernels  55.6 us (81%)
  local copies, waits for them, and re-layouts  10.3 us (15%)
  other arithmetic  2.63 us (4%)
    pallas_call x1, Pallas kernels, on_device(): pl.pallas_call(functools.partial(kernel, n, grid_n, loc_len, chunks), out...  55.6 us
    reshape x1, local copies, waits for them, and re-layouts, on_device(): return out.reshape(local, cols, variables)  4.14 us
    reshape x1, local copies, waits for them, and re-layouts, on_device(): background.reshape(local, width)  3.95 us
    unnamed x1, local copies, waits for them, and re-layouts  1.56 us

profile of v1, /device:TPU:1, one launch (start us, length us, event | category | flops | bytes accessed | tf_op | source)
XLA Modules:
  0.0 68.6 jit_solution(15014626700096033413)
XLA Ops:
  0.0 1.3 %add_divide_fusion.taper_ref = f32[4,4]{1,0:T(4,128)} fusion(s32[4,4]{1,0:T(4,128)} %loc_ref.1), kind=kLoop, calls=%fused_computation.5 | loop fusion | flops 64 | bytes 128 | tf_op jit(solution)/shard_map/div | solution.py:229
  1.3 0.7 reshape.9
  2.0 0.8 %convert_select_fusion = f32[4,256]{1,0:T(4,128)S(1)} fusion(bf16[4,256]{1,0:T(4,128)(2,1)} %param.8, s32[4]{0:T(128)} %param.9), kind=kLoop, calls=%fused_computation.3 | loop fusion | flops 3072 | bytes 6160 | tf_op jit(solution)/shard_map/jit(_where)/select_n | solution.py:226
  2.7 0.6 select_maximum_fusion.table_ref
  3.3 1.6 %copy.9 = bf16[64,4,256]{2,0,1:T(8,128)(2,1)} copy(bf16[64,4,256]{2,1,0:T(4,128)(2,1)} %param.6) | data formatting | bytes 262144 | tf_op args[0]
  4.9 3.9 %reshape.7.bg_ref = bf16[64,10240]{1,0:T(8,128)(2,1)} reshape(bf16[64,32,320]{2,1,0:T(8,128)(2,1)} %param.11) | data formatting | bytes 2621440 | tf_op jit(solution)/shard_map/reshape | solution.py:260
  8.8 55.6 %analysis.1 = bf16[64,10240]{1,0:T(8,128)(2,1)} custom-call(s32[4,4]{1,0:T(4,128)} %loc_ref.1, f32[4,4]{1,0:T(4,128)} %add_divide_fusion.taper_ref, bf16[4,64,256]{2,1,0:T(8,128)(2,1)} %bitcast.3, f32[4,8,256]{2,1,0:T(8,128)} %select_maximum_fusion.table_ref, bf16[64,10240]{1,0:T(8,128)(2,1)} %reshape.7.bg_ref), custom_call_target="tpu_custom_call" | custom-call | tf_op jit(solution)/shard_map/analysis/pallas_call | solution.py:233
  64.4 4.1 %reshape.8 = bf16[64,32,320]{2,1,0:T(8,128)(2,1)} reshape(bf16[64,10240]{1,0:T(8,128)(2,1)} %analysis.1) | data formatting | bytes 2621440 | tf_op jit(solution)/shard_map/reshape | solution.py:261
  (1 shorter events, 0.0 us)

commit v2 on v1

v2 whole, which is shorter than its diff:
```python
import functools

import jax
import jax.numpy as jnp
from jax import lax
from jax.experimental import pallas as pl
from jax.experimental.pallas import tpu as pltpu
from jax.sharding import PartitionSpec as P

REACH = 2
NS_STEPS = 6
PIECES = 2
EARLY = 5
MESH = pl.DeviceIdType.MESH
HIGHEST = lax.Precision.HIGHEST
NT = (((1,), (1,)), ((), ()))


def dot(a, b):
    return jnp.dot(a, b, precision=HIGHEST, preferred_element_type=jnp.float32)


def kernel(n, grid_n, loc_ref, counts_ref, obs_ref, values_ref, inverse_ref, bg_ref, out_ref,
           mine, near, own_table, tables, raw, state, upper, lower, sent_w, got_w, result,
           obs_send, obs_pass, obs_recv, tab_send, tab_recv, raw_sem, out_sem, direct_send, pair_send, pass_send,
           state_recv, w_send, w_recv):
    me = lax.axis_index("mem")
    row = lax.axis_index("grid")
    core = lax.rem(me, 2)
    chip = me // 2
    sibling = me + 1 - 2 * core
    rest = n // 2
    local, blocks, slots = obs_ref.shape
    cols, variables = bg_ref.shape[1:]
    members = n * local
    loc_len = loc_ref.shape[1]
    per = cols // blocks
    width = cols * variables
    chunks = PIECES * blocks
    step = width // chunks
    early = chunks * EARLY // 8
    around = 2 + 2 * REACH

    def at(mem, shift):
        return {"mem": mem, "grid": lax.rem(row + shift + grid_n, grid_n)}

    def rows_of(mem):
        return pl.ds(pl.multiple_of(mem * local, local), local)

    barrier = pltpu.get_barrier_semaphore()
    for shift in (0, -1, 1):
        for k in range(0 if shift else 1, n):
            pl.semaphore_signal(barrier, inc=1, device_id=at(lax.rem(me + k, n), shift), device_id_type=MESH)

    def raw_copy(b):
        part = pl.ds(b * per, per)
        return pltpu.make_async_copy(bg_ref.at[:, part], raw.at[:, part], raw_sem.at[b])

    def out_copy(b):
        part = pl.ds(b * per, per)
        return pltpu.make_async_copy(result.at[:, part], out_ref.at[:, part], out_sem.at[b])

    for b in range(blocks):
        raw_copy(b).start()
    mine[...] = jnp.swapaxes(obs_ref[...].astype(jnp.float32), 0, 1).astype(jnp.bfloat16)
    values = values_ref[...].astype(jnp.float32)
    inverse = inverse_ref[...].astype(jnp.float32)
    lane = lax.broadcasted_iota(jnp.int32, (1, slots), 1)
    upmost = lax.broadcasted_iota(jnp.int32, (8, slots), 0) == 0
    for b in range(blocks):
        masked = jnp.where(lane < counts_ref[b], inverse[b : b + 1], 0.0)
        entry = jnp.where(upmost, values[b : b + 1], masked)
        own_table[b] = entry
        tables[blocks + b] = entry
    own_rows = rows_of(me)
    pl.semaphore_wait(barrier, 3 * n - 1)

    def obs_copy(i, q):
        return pltpu.make_async_remote_copy(
            src_ref=mine.at[i], dst_ref=near.at[i - 2 * q + REACH, own_rows],
            send_sem=obs_send.at[i, q + 1], recv_sem=obs_recv.at[i - 2 * q + REACH, me],
            device_id=at(2 * (q % rest) + core, q // rest), device_id_type=MESH)

    def own_obs(i, q):
        u = i - 2 * q + REACH
        return pltpu.make_async_copy(mine.at[i], near.at[u, own_rows], obs_recv.at[u, me])

    def obs_passed(u, k):
        rows = rows_of(2 * k + core)
        return pltpu.make_async_remote_copy(
            src_ref=near.at[u, rows], dst_ref=near.at[u, rows],
            send_sem=obs_pass.at[u, k], recv_sem=obs_recv.at[u, 2 * k + core],
            device_id=at(sibling, 0), device_id_type=MESH)

    def await_obs(u, mem):
        ref = near.at[u, rows_of(mem)]
        pltpu.make_async_copy(ref, ref, obs_recv.at[u, mem]).wait()

    def table_copy(side):
        place = 0 if side == 1 else 2 * blocks
        return pltpu.make_async_remote_copy(
            src_ref=own_table, dst_ref=tables.at[pl.ds(place, blocks)],
            send_sem=tab_send.at[(side + 1) // 2], recv_sem=tab_recv.at[(side + 1) // 2],
            device_id=at(me, side), device_id_type=MESH)

    targets = [(i, q) for i in range(blocks) for q in range(-1, rest + 1) if 0 <= i - 2 * q + REACH < around]
    targets.sort(key=lambda t: 0 <= t[1] < rest)
    for i, q in targets:
        if 0 <= q < rest:
            @pl.when(chip != q)
            def _():
                obs_copy(i, q).start()

            @pl.when(chip == q)
            def _():
                own_obs(i, q).start()
        else:
            obs_copy(i, q).start()
    for side in (-1, 1):
        table_copy(side).start()

    def piece(j):
        return pl.ds(j * step, step)

    def direct(k, j):
        part = state.at[own_rows, piece(j)]
        return pltpu.make_async_remote_copy(
            src_ref=part, dst_ref=part, send_sem=direct_send.at[k, j], recv_sem=state_recv.at[me, j],
            device_id=at(lax.rem(me + 2 * k, n), 0), device_id_type=MESH)

    def paired(j):
        part = state.at[own_rows, piece(j)]
        return pltpu.make_async_remote_copy(
            src_ref=part, dst_ref=part, send_sem=pair_send.at[j], recv_sem=state_recv.at[me, j],
            device_id=at(sibling, 0), device_id_type=MESH)

    def passed(k, j):
        source = lax.rem(me + n - 2 * k, n)
        part = state.at[rows_of(source), piece(j)]
        return pltpu.make_async_remote_copy(
            src_ref=part, dst_ref=part, send_sem=pass_send.at[k, j], recv_sem=state_recv.at[source, j],
            device_id=at(sibling, 0), device_id_type=MESH)

    def await_state(source, j):
        ref = state.at[rows_of(source), piece(j)]
        pltpu.make_async_copy(ref, ref, state_recv.at[source, j]).wait()

    def send_state(j):
        for k in range(1, rest):
            direct(k, j).start()
        paired(j).start()

    for b in range(blocks):
        raw_copy(b).wait()
        whole = raw[:, b * per : (b + 1) * per].astype(jnp.float32)
        by_col = jnp.swapaxes(whole, 0, 1).astype(jnp.bfloat16)
        state[own_rows, b * per * variables : (b + 1) * per * variables] = jnp.concatenate(
            [by_col[c] for c in range(per)], axis=1)
        for j in range(b * PIECES, (b + 1) * PIECES):
            if j < early:
                send_state(j)

    for u in range(around):
        for k in range(rest):
            await_obs(u, 2 * k + core)
            obs_passed(u, k).start()
    for side in (-1, 1):
        table_copy(side).wait_recv()
    for u in range(around):
        for k in range(rest):
            await_obs(u, 2 * k + 1 - core)

    gram = jnp.zeros((members, members), jnp.float32)
    rhs = jnp.zeros((8, members), jnp.float32)
    for j in range(loc_len):
        offset = loc_ref[me, j]
        wide = near[core + offset + REACH].astype(jnp.float32)
        table = tables[blocks + me + offset]
        distance = jnp.abs(jnp.full((1, slots), offset, jnp.int32)).astype(jnp.float32)
        weight = table[1:2] * (1.0 / (1.0 + distance))
        mean = jnp.sum(wide, axis=0, keepdims=True) * (1.0 / members)
        scaled = ((wide - mean) * weight).astype(jnp.bfloat16)
        innovation = jnp.broadcast_to((table[0:1] - mean) * weight, (8, slots))
        gram = gram + lax.dot_general(scaled, scaled, NT, preferred_element_type=jnp.float32)
        rhs = rhs + lax.dot_general(innovation, scaled.astype(jnp.float32), NT, precision=HIGHEST,
                                    preferred_element_type=jnp.float32)
    across = lax.broadcasted_iota(jnp.int32, (members, members), 0)
    along = lax.broadcasted_iota(jnp.int32, (members, members), 1)
    identity = (across == along).astype(jnp.float32)
    system = identity + gram / (members - 1)
    square = jnp.sum(jnp.sum(system * system, axis=1, keepdims=True), axis=0, keepdims=True)
    scale = jnp.sqrt(square)
    first = system / scale
    middle = 0.5 * (3.0 * identity - first)
    upper[...] = dot(first, middle)
    lower[...] = middle

    def newton(_, carry):
        mid = 1.5 * identity - 0.5 * dot(lower[...], upper[...])
        upper[...] = dot(upper[...], mid)
        lower[...] = dot(mid, lower[...])
        return carry

    lax.fori_loop(0, NS_STEPS - 2, newton, 0)
    middle = 1.5 * identity - 0.5 * dot(lower[...], upper[...])
    root_inv = dot(middle, lower[...]) / jnp.sqrt(scale)
    shift = dot(dot(rhs, root_inv), root_inv) / (members - 1)
    sent_w[...] = (root_inv + shift[0:1]).astype(jnp.bfloat16)

    def weight_copy(k):
        peer = lax.rem(me + k, n)
        return pltpu.make_async_remote_copy(
            src_ref=sent_w.at[rows_of(peer)], dst_ref=got_w.at[me],
            send_sem=w_send.at[k], recv_sem=w_recv.at[me], device_id=at(peer, 0), device_id_type=MESH)

    for k in range(1, rest):
        await_state(lax.rem(me + n - 2 * k, n), 0)
        passed(k, 0).start()
    for k in range(1, n):
        weight_copy(k).start()
    pltpu.make_async_copy(sent_w.at[own_rows], got_w.at[me], w_recv.at[me]).start()
    for j in range(early, chunks):
        send_state(j)
    for source in range(n):
        pltpu.make_async_copy(got_w.at[source], got_w.at[source], w_recv.at[source]).wait()

    for b in range(blocks):
        weights = got_w[b].astype(jnp.float32)
        folded = weights - jnp.sum(weights, axis=1, keepdims=True) * (1.0 / members) + 1.0 / members
        high = folded.astype(jnp.bfloat16)
        low = (folded - high.astype(jnp.float32)).astype(jnp.bfloat16)
        for j in range(b * PIECES, (b + 1) * PIECES):
            if j + 1 < chunks:
                for k in range(1, rest):
                    await_state(lax.rem(me + n - 2 * k, n), j + 1)
                    passed(k, j + 1).start()
            await_state(sibling, j)
            for k in range(1, rest):
                await_state(lax.rem(sibling + n - 2 * k, n), j)
        block_state = state[:, b * per * variables : (b + 1) * per * variables]
        total = jnp.dot(high, block_state, preferred_element_type=jnp.float32)
        total = total + jnp.dot(low, block_state, preferred_element_type=jnp.float32)
        by_col = jnp.stack([total[:, c * variables : (c + 1) * variables] for c in range(per)], axis=0)
        result[:, b * per : (b + 1) * per] = jnp.swapaxes(by_col, 0, 1).astype(jnp.bfloat16)
        out_copy(b).start()

    for i, q in targets:
        if 0 <= q < rest:
            @pl.when(chip != q)
            def _():
                obs_copy(i, q).wait_send()
        else:
            obs_copy(i, q).wait_send()
    for u in range(around):
        for k in range(rest):
            obs_passed(u, k).wait_send()
    for side in (-1, 1):
        table_copy(side).wait_send()
    for k in range(1, n):
        weight_copy(k).wait_send()
    for j in range(chunks):
        paired(j).wait_send()
        for k in range(1, rest):
            direct(k, j).wait_send()
            passed(k, j).wait_send()
    for b in range(blocks):
        out_copy(b).wait()


def on_device(n, grid_n, obs_ensemble, obs_values, inverse_error, obs_counts, loc_offsets, background):
    local, blocks, slots = obs_ensemble.shape
    cols, variables = background.shape[1:]
    members = n * local
    width = cols * variables
    chunks = PIECES * blocks
    rest = n // 2
    around = 2 + 2 * REACH
    assert blocks == n and n % 2 == 0
    dma = pltpu.SemaphoreType.DMA
    smem = pl.BlockSpec(memory_space=pltpu.SMEM)
    vmem = pl.BlockSpec(memory_space=pltpu.VMEM)
    whole = pl.BlockSpec(memory_space=pl.ANY)
    return pl.pallas_call(
        functools.partial(kernel, n, grid_n),
        out_shape=jax.ShapeDtypeStruct((local, cols, variables), jnp.bfloat16),
        in_specs=[smem, smem, vmem, vmem, vmem, whole],
        out_specs=whole,
        scratch_shapes=[
            pltpu.VMEM((blocks, local, slots), jnp.bfloat16),
            pltpu.VMEM((around, members, slots), jnp.bfloat16),
            pltpu.VMEM((blocks, 8, slots), jnp.float32),
            pltpu.VMEM((3 * blocks, 8, slots), jnp.float32),
            pltpu.VMEM((local, cols, variables), jnp.bfloat16),
            pltpu.VMEM((members, width), jnp.bfloat16),
            pltpu.VMEM((members, members), jnp.float32),
            pltpu.VMEM((members, members), jnp.float32),
            pltpu.VMEM((members, members), jnp.bfloat16),
            pltpu.VMEM((n, local, members), jnp.bfloat16),
            pltpu.VMEM((local, cols, variables), jnp.bfloat16),
            dma((blocks, rest + 2)),
            dma((around, rest)),
            dma((around, n)),
            dma((2,)),
            dma((2,)),
            dma((blocks,)),
            dma((blocks,)),
            dma((rest, chunks)),
            dma((chunks,)),
            dma((rest, chunks)),
            dma((n, chunks)),
            dma((n,)),
            dma((n,)),
        ],
        compiler_params=pltpu.CompilerParams(collective_id=0, has_side_effects=True, vmem_limit_bytes=60 * 2**20),
        name="analysis",
    )(loc_offsets, obs_counts, obs_ensemble, obs_values, inverse_error, background)


def solution(mesh):
    placed = (
        P("mem", "grid", None),
        P("grid", None),
        P("grid", None),
        P("grid"),
        P("grid", None),
        P("mem", "grid", None),
    )
    body = functools.partial(on_device, mesh.shape["mem"], mesh.shape["grid"])
    return jax.shard_map(body, mesh=mesh, in_specs=placed, out_specs=P("mem", "grid", None), check_vma=False)
```

time: 68.9 us -> 49.8 us (0.72)
  Pallas kernels: 55.6 us -> 47 us
  local copies, waits for them, and re-layouts: 10.3 us -> 2.71 us
  other arithmetic: 2.63 us -> 0 us
    pallas_call x1, Pallas kernels: 55.6 us -> 47 us  [on_device(): pl.pallas_call(functools.partial(kernel, n, grid_n), out_shape=jax.ShapeD...]
    reshape x2 -> x0, local copies, waits for them, and re-layouts: 8.09 us -> none  [the longest x1 4.14 us: on_device(): return out.reshape(local, cols, variables)]
    div x1 -> x0, other arithmetic: 1.27 us -> none  [on_device(): taper = 1.0 / (1.0 + jnp.abs(loc_offsets).astype(jnp.float32))]
    unnamed x1, local copies, waits for them, and re-layouts: 1.56 us -> 2.71 us
    select_n x1 -> x0, other arithmetic: 0.75 us -> none  [on_device(): jnp.where(slot_ids[None, :] < obs_counts[:, None], inverse_error.astype(j...]
    another operation x2 -> x0, local copies, waits for them, and re-layouts: 0.69 us -> none  [on_device(): table = jnp.stack([obs_values.astype(jnp.float32), masked], axis=1)]
where the time goes in v2:
time: 49.8 us; the launch traced here: 49.7 us
  Pallas kernels  47 us (94%)
  local copies, waits for them, and re-layouts  2.71 us (5%)
    pallas_call x1, Pallas kernels, on_device(): pl.pallas_call(functools.partial(kernel, n, grid_n), out_shape=jax.ShapeD...  47 us
    unnamed x1, local copies, waits for them, and re-layouts  2.71 us

profile of v2, /device:TPU:1, one launch (start us, length us, event | category | flops | bytes accessed | tf_op | source)
XLA Modules:
  0.0 49.7 jit_solution(936404070078522479)
XLA Ops:
  0.0 47.0 %analysis.1 = bf16[64,32,320]{2,1,0:T(8,128)(2,1)} custom-call(s32[4,4]{1,0:T(4,128)} %loc_ref.1, s32[4]{0:T(128)} %counts_ref.1, bf16[64,4,256]{2,1,0:T(4,128)(2,1)} %obs_ref.1, bf16[4,256]{1,0:T(4,128)(2,1)} %values_ref.1, bf16[4,256]{1,0:T(4,128)(2,1)} %inverse_ref.1, bf16[64,32,320]{2,1,0:T(8,128)(2,1)} %bg_ref.1), custom_call_target="tpu_custom_call" | custom-call | tf_op jit(solution)/shard_map/analysis/pallas_call | solution.py:283
  47.0 2.7 %copy.8 = bf16[64,32,320]{2,1,0:T(8,128)(2,1)} copy(bf16[64,32,320]{2,1,0:T(8,128)(2,1)} %analysis.1) | data formatting | bytes 2621440

commit v3 on v2

--- a/solution.py
+++ b/solution.py
@@ -10,7 +10,9 @@
 REACH = 2
 NS_STEPS = 6
 PIECES = 2
+FIRST = 2
 EARLY = 5
+HUB = 0
 MESH = pl.DeviceIdType.MESH
 HIGHEST = lax.Precision.HIGHEST
 NT = (((1,), (1,)), ((), ()))
@@ -20,9 +22,9 @@
     return jnp.dot(a, b, precision=HIGHEST, preferred_element_type=jnp.float32)
 
 
-def kernel(n, grid_n, loc_ref, counts_ref, obs_ref, values_ref, inverse_ref, bg_ref, out_ref,
-           mine, near, own_table, tables, raw, state, upper, lower, sent_w, got_w, result,
-           obs_send, obs_pass, obs_recv, tab_send, tab_recv, raw_sem, out_sem, direct_send, pair_send, pass_send,
+def kernel(n, grid_n, loc_ref, counts_ref, obs_ref, values_ref, inverse_ref, bg_ref, result,
+           mine, near, own_table, tables, raw, state, upper, lower, sent_w, got_w, group_sem, cross_sem,
+           obs_send, obs_pass, obs_recv, tab_send, tab_recv, raw_sem, direct_send, pair_send, pass_send,
            state_recv, w_send, w_recv):
     me = lax.axis_index("mem")
     row = lax.axis_index("grid")
@@ -38,6 +40,7 @@
     width = cols * variables
     chunks = PIECES * blocks
     step = width // chunks
+    initial = chunks * FIRST // 8
     early = chunks * EARLY // 8
     around = 2 + 2 * REACH
 
@@ -48,17 +51,15 @@
         return pl.ds(pl.multiple_of(mem * local, local), local)
 
     barrier = pltpu.get_barrier_semaphore()
-    for shift in (0, -1, 1):
-        for k in range(0 if shift else 1, n):
-            pl.semaphore_signal(barrier, inc=1, device_id=at(lax.rem(me + k, n), shift), device_id_type=MESH)
+    for p in range(n):
+        if p != HUB:
+            @pl.when(me != p)
+            def _():
+                pl.semaphore_signal(barrier, inc=1, device_id=at(p, 0), device_id_type=MESH)
 
     def raw_copy(b):
         part = pl.ds(b * per, per)
         return pltpu.make_async_copy(bg_ref.at[:, part], raw.at[:, part], raw_sem.at[b])
-
-    def out_copy(b):
-        part = pl.ds(b * per, per)
-        return pltpu.make_async_copy(result.at[:, part], out_ref.at[:, part], out_sem.at[b])
 
     for b in range(blocks):
         raw_copy(b).start()
@@ -73,7 +74,18 @@
         own_table[b] = entry
         tables[blocks + b] = entry
     own_rows = rows_of(me)
-    pl.semaphore_wait(barrier, 3 * n - 1)
+
+    @pl.when(me != HUB)
+    def _():
+        pl.semaphore_wait(barrier, n - 1)
+        pl.semaphore_signal(group_sem, inc=1, device_id=at(HUB, 0), device_id_type=MESH)
+
+    @pl.when(me == HUB)
+    def _():
+        pl.semaphore_wait(group_sem, n - 1)
+        for side in (-1, 1):
+            pl.semaphore_signal(barrier, inc=1, device_id=at(HUB, side), device_id_type=MESH)
+
 
     def obs_copy(i, q):
         return pltpu.make_async_remote_copy(
@@ -104,7 +116,6 @@
             device_id=at(me, side), device_id_type=MESH)
 
     targets = [(i, q) for i in range(blocks) for q in range(-1, rest + 1) if 0 <= i - 2 * q + REACH < around]
-    targets.sort(key=lambda t: 0 <= t[1] < rest)
     for i, q in targets:
         if 0 <= q < rest:
             @pl.when(chip != q)
@@ -114,10 +125,6 @@
             @pl.when(chip == q)
             def _():
                 own_obs(i, q).start()
-        else:
-            obs_copy(i, q).start()
-    for side in (-1, 1):
-        table_copy(side).start()
 
     def piece(j):
         return pl.ds(j * step, step)
@@ -152,13 +159,30 @@
 
     for b in range(blocks):
         raw_copy(b).wait()
-        whole = raw[:, b * per : (b + 1) * per].astype(jnp.float32)
-        by_col = jnp.swapaxes(whole, 0, 1).astype(jnp.bfloat16)
-        state[own_rows, b * per * variables : (b + 1) * per * variables] = jnp.concatenate(
-            [by_col[c] for c in range(per)], axis=1)
+        state[own_rows, b * per * variables : (b + 1) * per * variables] = (
+            raw[:, b * per : (b + 1) * per].reshape(local, per * variables))
         for j in range(b * PIECES, (b + 1) * PIECES):
-            if j < early:
+            if j < initial:
                 send_state(j)
+
+    @pl.when(me == HUB)
+    def _():
+        pl.semaphore_wait(barrier, 2)
+        for p in range(n):
+            if p != HUB:
+                pl.semaphore_signal(cross_sem, inc=1, device_id=at(p, 0), device_id_type=MESH)
+
+    @pl.when(me != HUB)
+    def _():
+        pl.semaphore_wait(cross_sem, 1)
+
+    for i, q in targets:
+        if not 0 <= q < rest:
+            obs_copy(i, q).start()
+    for side in (-1, 1):
+        table_copy(side).start()
+    for j in range(initial, early):
+        send_state(j)
 
     for u in range(around):
         for k in range(rest):
@@ -240,9 +264,7 @@
         block_state = state[:, b * per * variables : (b + 1) * per * variables]
         total = jnp.dot(high, block_state, preferred_element_type=jnp.float32)
         total = total + jnp.dot(low, block_state, preferred_element_type=jnp.float32)
-        by_col = jnp.stack([total[:, c * variables : (c + 1) * variables] for c in range(per)], axis=0)
-        result[:, b * per : (b + 1) * per] = jnp.swapaxes(by_col, 0, 1).astype(jnp.bfloat16)
-        out_copy(b).start()
+        result[:, b * per * variables : (b + 1) * per * variables] = total.astype(jnp.bfloat16)
 
     for i, q in targets:
         if 0 <= q < rest:
@@ -263,8 +285,20 @@
         for k in range(1, rest):
             direct(k, j).wait_send()
             passed(k, j).wait_send()
-    for b in range(blocks):
-        out_copy(b).wait()
+
+
+def spread(blocks, flat_ref, out_ref, columns, sems):
+    local, cols, variables = out_ref.shape
+    per = cols // blocks
+    copies = []
+    for b in range(blocks):
+        part = pl.ds(b * per, per)
+        columns[:, b * per : (b + 1) * per] = (
+            flat_ref[:, b * per * variables : (b + 1) * per * variables].reshape(local, per, variables))
+        copies.append(pltpu.make_async_copy(columns.at[:, part], out_ref.at[:, part], sems.at[b]))
+        copies[-1].start()
+    for copy in copies:
+        copy.wait()
 
 
 def on_device(n, grid_n, obs_ensemble, obs_values, inverse_error, obs_counts, loc_offsets, background):
@@ -280,11 +314,11 @@
     smem = pl.BlockSpec(memory_space=pltpu.SMEM)
     vmem = pl.BlockSpec(memory_space=pltpu.VMEM)
     whole = pl.BlockSpec(memory_space=pl.ANY)
-    return pl.pallas_call(
+    flat = pl.pallas_call(
         functools.partial(kernel, n, grid_n),
-        out_shape=jax.ShapeDtypeStruct((local, cols, variables), jnp.bfloat16),
+        out_shape=pltpu.VMEM((local, width), jnp.bfloat16),
         in_specs=[smem, smem, vmem, vmem, vmem, whole],
-        out_specs=whole,
+        out_specs=vmem,
         scratch_shapes=[
             pltpu.VMEM((blocks, local, slots), jnp.bfloat16),
             pltpu.VMEM((around, members, slots), jnp.bfloat16),
@@ -296,13 +330,13 @@
             pltpu.VMEM((members, members), jnp.float32),
             pltpu.VMEM((members, members), jnp.bfloat16),
             pltpu.VMEM((n, local, members), jnp.bfloat16),
-            pltpu.VMEM((local, cols, variables), jnp.bfloat16),
+            pltpu.SemaphoreType.REGULAR,
+            pltpu.SemaphoreType.REGULAR,
             dma((blocks, rest + 2)),
             dma((around, rest)),
             dma((around, n)),
             dma((2,)),
             dma((2,)),
-            dma((blocks,)),
             dma((blocks,)),
             dma((rest, chunks)),
             dma((chunks,)),
@@ -314,6 +348,15 @@
         compiler_params=pltpu.CompilerParams(collective_id=0, has_side_effects=True, vmem_limit_bytes=60 * 2**20),
         name="analysis",
     )(loc_offsets, obs_counts, obs_ensemble, obs_values, inverse_error, background)
+    return pl.pallas_call(
+        functools.partial(spread, blocks),
+        out_shape=jax.ShapeDtypeStruct((local, cols, variables), jnp.bfloat16),
+        in_specs=[vmem],
+        out_specs=whole,
+        scratch_shapes=[pltpu.VMEM((local, cols, variables), jnp.bfloat16), dma((blocks,))],
+        compiler_params=pltpu.CompilerParams(vmem_limit_bytes=16 * 2**20),
+        name="spread",
+    )(flat)
 
 
 def solution(mesh):

time: 49.8 us -> 44.9 us (0.902)
  local copies, waits for them, and re-layouts: 2.71 us -> 0 us
  Pallas kernels: 47 us -> 44.4 us
    unnamed x1 -> x0, local copies, waits for them, and re-layouts: 2.71 us -> none
    pallas_call x1 -> x2, Pallas kernels: 47 us -> 44.4 us  [the longest x1 43 us: on_device(): pl.pallas_call(functools.partial(kernel, n, grid_n), out_shape=pltpu.VMEM...]
where the time goes in v3:
time: 44.9 us; the launch traced here: 44.4 us
  Pallas kernels  44.4 us (99%)
    pallas_call x1, Pallas kernels, on_device(): pl.pallas_call(functools.partial(kernel, n, grid_n), out_shape=pltpu.VMEM...  43 us
    pallas_call x1, Pallas kernels, on_device(): pl.pallas_call(functools.partial(spread, blocks), out_shape=jax.ShapeDtyp...  1.36 us

profile of v3, /device:TPU:1, one launch (start us, length us, event | category | flops | bytes accessed | tf_op | source)
XLA Modules:
  0.0 44.4 jit_solution(17037078061222518791)
XLA Ops:
  0.0 43.0 %analysis.1.flat_ref = bf16[64,10240]{1,0:T(8,128)(2,1)S(1)} custom-call(s32[4,4]{1,0:T(4,128)} %loc_ref.1, s32[4]{0:T(128)} %counts_ref.1, bf16[64,4,256]{2,1,0:T(4,128)(2,1)} %obs_ref.1, bf16[4,256]{1,0:T(4,128)(2,1)} %values_ref.1, bf16[4,256]{1,0:T(4,128)(2,1)} %inverse_ref.1, bf16[64,32,320]{2,1,0:T(8,128)(2,1)} %bg_ref.1), custom_call_target="tpu_custom_call" | custom-call | tf_op jit(solution)/shard_map/analysis/pallas_call | solution.py:317
  43.0 1.4 %spread.1 = bf16[64,32,320]{2,1,0:T(8,128)(2,1)} custom-call(bf16[64,10240]{1,0:T(8,128)(2,1)S(1)} %analysis.1.flat_ref), custom_call_target="tpu_custom_call" | custom-call | tf_op jit(solution)/shard_map/spread/pallas_call | solution.py:351

commit v4 on v3

--- a/solution.py
+++ b/solution.py
@@ -11,7 +11,7 @@
 NS_STEPS = 6
 PIECES = 2
 FIRST = 2
-EARLY = 5
+EARLY = 6
 HUB = 0
 MESH = pl.DeviceIdType.MESH
 HIGHEST = lax.Precision.HIGHEST
@@ -253,6 +253,7 @@
         folded = weights - jnp.sum(weights, axis=1, keepdims=True) * (1.0 / members) + 1.0 / members
         high = folded.astype(jnp.bfloat16)
         low = (folded - high.astype(jnp.float32)).astype(jnp.bfloat16)
+        parts = []
         for j in range(b * PIECES, (b + 1) * PIECES):
             if j + 1 < chunks:
                 for k in range(1, rest):
@@ -261,10 +262,11 @@
             await_state(sibling, j)
             for k in range(1, rest):
                 await_state(lax.rem(sibling + n - 2 * k, n), j)
-        block_state = state[:, b * per * variables : (b + 1) * per * variables]
-        total = jnp.dot(high, block_state, preferred_element_type=jnp.float32)
-        total = total + jnp.dot(low, block_state, preferred_element_type=jnp.float32)
-        result[:, b * per * variables : (b + 1) * per * variables] = total.astype(jnp.bfloat16)
+            piece_state = state[:, j * step : (j + 1) * step]
+            total = jnp.dot(high, piece_state, preferred_element_type=jnp.float32)
+            total = total + jnp.dot(low, piece_state, preferred_element_type=jnp.float32)
+            parts.append(total.astype(jnp.bfloat16))
+        result[:, b * per : (b + 1) * per] = jnp.concatenate(parts, axis=1).reshape(local, per, variables)
 
     for i, q in targets:
         if 0 <= q < rest:
@@ -287,16 +289,12 @@
             passed(k, j).wait_send()
 
 
-def spread(blocks, flat_ref, out_ref, columns, sems):
-    local, cols, variables = out_ref.shape
-    per = cols // blocks
-    copies = []
-    for b in range(blocks):
-        part = pl.ds(b * per, per)
-        columns[:, b * per : (b + 1) * per] = (
-            flat_ref[:, b * per * variables : (b + 1) * per * variables].reshape(local, per, variables))
-        copies.append(pltpu.make_async_copy(columns.at[:, part], out_ref.at[:, part], sems.at[b]))
-        copies[-1].start()
+def spread(blocks, held_ref, out_ref, sems):
+    per = out_ref.shape[1] // blocks
+    parts = [pl.ds(b * per, per) for b in range(blocks)]
+    copies = [pltpu.make_async_copy(held_ref.at[:, p], out_ref.at[:, p], sems.at[b]) for b, p in enumerate(parts)]
+    for copy in copies:
+        copy.start()
     for copy in copies:
         copy.wait()
 
@@ -314,9 +312,9 @@
     smem = pl.BlockSpec(memory_space=pltpu.SMEM)
     vmem = pl.BlockSpec(memory_space=pltpu.VMEM)
     whole = pl.BlockSpec(memory_space=pl.ANY)
-    flat = pl.pallas_call(
+    held = pl.pallas_call(
         functools.partial(kernel, n, grid_n),
-        out_shape=pltpu.VMEM((local, width), jnp.bfloat16),
+        out_shape=pltpu.VMEM((local, cols, variables), jnp.bfloat16),
         in_specs=[smem, smem, vmem, vmem, vmem, whole],
         out_specs=vmem,
         scratch_shapes=[
@@ -353,10 +351,10 @@
         out_shape=jax.ShapeDtypeStruct((local, cols, variables), jnp.bfloat16),
         in_specs=[vmem],
         out_specs=whole,
-        scratch_shapes=[pltpu.VMEM((local, cols, variables), jnp.bfloat16), dma((blocks,))],
+        scratch_shapes=[dma((blocks,))],
         compiler_params=pltpu.CompilerParams(vmem_limit_bytes=16 * 2**20),
         name="spread",
-    )(flat)
+    )(held)
 
 
 def solution(mesh):

time: 44.9 us -> 43.1 us (0.960)
  Pallas kernels: 44.4 us -> 42.9 us
    pallas_call x1, Pallas kernels: 43 us -> 41.7 us  [on_device(): pl.pallas_call(functools.partial(kernel, n, grid_n), out_shape=pltpu.VMEM...]
where the time goes in v4:
time: 43.1 us; the launch traced here: 42.9 us
  Pallas kernels  42.9 us (100%)
    pallas_call x1, Pallas kernels, on_device(): pl.pallas_call(functools.partial(kernel, n, grid_n), out_shape=pltpu.VMEM...  41.7 us
    pallas_call x1, Pallas kernels, on_device(): pl.pallas_call(functools.partial(spread, blocks), out_shape=jax.ShapeDtyp...  1.17 us

profile of v4, /device:TPU:1, one launch (start us, length us, event | category | flops | bytes accessed | tf_op | source)
XLA Modules:
  0.0 42.9 jit_solution(15302189877968403736)
XLA Ops:
  0.0 41.7 %analysis.1.held_ref = bf16[64,32,320]{2,1,0:T(8,128)(2,1)S(1)} custom-call(s32[4,4]{1,0:T(4,128)} %loc_ref.1, s32[4]{0:T(128)} %counts_ref.1, bf16[64,4,256]{2,1,0:T(4,128)(2,1)} %obs_ref.1, bf16[4,256]{1,0:T(4,128)(2,1)} %values_ref.1, bf16[4,256]{1,0:T(4,128)(2,1)} %inverse_ref.1, bf16[64,32,320]{2,1,0:T(8,128)(2,1)} %bg_ref.1), custom_call_target="tpu_custom_call" | custom-call | tf_op jit(solution)/shard_map/analysis/pallas_call | solution.py:315
  41.7 1.2 %spread.1 = bf16[64,32,320]{2,1,0:T(8,128)(2,1)} custom-call(bf16[64,32,320]{2,1,0:T(8,128)(2,1)S(1)} %analysis.1.held_ref), custom_call_target="tpu_custom_call" | custom-call | tf_op jit(solution)/shard_map/spread/pallas_call | solution.py:349
